TPU v7x, 512 devices: a whole 4x4x16 slice. The times are simulated.
512 devices in a mesh: ctx: 32 (over z, x_lo), zero: 16 (over x_hi, y, core).
Axes of the slice: x: 4 (x_hi: 2, x_lo: 2; x = x_hi * 2 + x_lo), y: 4, z: 16, core: 2. Of those that a mesh axis runs over, the one named last changes fastest.
Arguments:
- activations: bfloat16 [16384, 4096], P('ctx', 'zero'), may hold values from -1200 to 1200
- norm_gain: bfloat16 [4096], replicated, may hold values from 0.099609375 to 1.8984375
- query_weight: bfloat16 [4096, 4096], P('ctx', 'zero'), may hold values from -24 to 24
- kv_weight: bfloat16 [4096, 16, 128], P('ctx', 'zero'), may hold values from -1 to 1
- out_weight: bfloat16 [4096, 4096], P('zero', 'ctx'), may hold values from -0.09375 to 0.09375
- tile_mask: int32 [32, 4, 4], P('ctx'), may hold values from 0 to 1, as said below
- anchor_mask: int32 [32, 4, 4], P('ctx'), may hold values 0 or 1
- anchor_index: int32 [1], replicated, may hold values from 0 to 31
Outputs:
- mixed: bfloat16 [16384, 4096], P(('ctx', 'zero'))
Inputs may be any that keep to these rules, and one draw needn't show every extreme that they name: `tile_mask`: entries of every block's table above the diagonal are 0 and diagonal entries are 1.
All inputs are finite; a program needn't handle non-finite values. No bound on the sum of `anchor_mask` on one device may be relied on, other than what follows from the above.
Results may differ from a plain program's by a relative error of at most 0.02.
Values may be sent and summed in bfloat16 or wider, within the bound.
A program may use at most 64 MiB of HBM per device.

v0:
```python
import jax
import jax.numpy as jnp
from jax import lax
from jax.sharding import PartitionSpec as P


def from_partner(value, axis, stride):
    mask = 2**stride
    pairs = [(source, source ^ mask) for source in range(lax.axis_size(axis))]
    return lax.ppermute(value, axis, pairs)


def from_root(block, axis, holder):
    block = jnp.where(lax.axis_index(axis) == holder, block, jnp.zeros_like(block))
    return lax.psum(block, axis)


def rotate(vectors, positions):
    half_size = vectors.shape[-1] // 2
    frequency = jnp.power(
        jnp.float32(500000.0), -(jnp.arange(half_size, dtype=jnp.float32) * 2.0 / vectors.shape[-1])
    )
    angles = positions.astype(jnp.float32)[:, None] * frequency[None, :]
    cosine_table = jnp.cos(angles)[:, None, :]
    sine_table = jnp.sin(angles)[:, None, :]
    first = vectors[..., :half_size]
    second = vectors[..., half_size:]
    return jnp.concatenate(
        [first * cosine_table - second * sine_table, second * cosine_table + first * sine_table], -1
    )


def expand_tiles(table, tile_size):
    tiles = table.shape[0]
    return jnp.broadcast_to(table[:, None, :, None], (tiles, tile_size, tiles, tile_size)).reshape(
        tiles * tile_size, tiles * tile_size
    )


def local(
    activations,
    norm_gain,
    query_weight,
    kv_weight,
    out_weight,
    tile_mask,
    anchor_mask,
    anchor_index,
):
    block_rows = activations.shape[0]
    head_size = kv_weight.shape[2]
    zero_rank = lax.axis_index("zero")
    ctx_rank = lax.axis_index("ctx")
    gain_float = norm_gain.astype(jnp.float32)
    gathered = lax.all_gather(activations, "zero", axis=1, tiled=True)
    x_float = gathered.astype(jnp.float32)
    mean_square = jnp.mean(x_float * x_float, -1, keepdims=True)
    normed = (x_float * lax.rsqrt(mean_square + 1e-05) * gain_float).astype(jnp.bfloat16)
    kv_rows_local = kv_weight[:, 0, :]

    def add_one(piece_rows):
        return jnp.dot(normed, piece_rows, preferred_element_type=jnp.float32)

    query_linear = add_one(lax.all_gather(query_weight, "ctx", axis=0, tiled=True))
    kv_linear = add_one(lax.all_gather(kv_rows_local, "ctx", axis=0, tiled=True))
    positions = ctx_rank * block_rows + jnp.arange(block_rows, dtype=jnp.int32)
    queries = (
        rotate(query_linear.reshape(block_rows, -1, head_size), positions) * head_size ** (-0.5)
    ).astype(jnp.bfloat16)
    is_key = zero_rank % 2 == 0
    own_half = jnp.where(
        is_key, rotate(kv_linear[:, None, :], positions)[:, 0, :], kv_linear
    ).astype(jnp.bfloat16)
    partner = from_partner(own_half, "zero", 0)
    own_keys = jnp.where(is_key, own_half, partner)
    own_values = jnp.where(is_key, partner, own_half)
    anchor_block = anchor_index[0]
    anchor_pair = from_root(jnp.stack([own_keys, own_values]), "ctx", anchor_block)
    all_keys = jnp.concatenate([anchor_pair[0], own_keys], 0)
    all_values = jnp.concatenate([anchor_pair[1], own_values], 0)
    scores = jnp.einsum("thd,kd->htk", queries, all_keys, preferred_element_type=jnp.float32)
    tile_size = block_rows // tile_mask.shape[1]
    row_offsets = jnp.arange(block_rows, dtype=jnp.int32)
    far_visible = (expand_tiles(anchor_mask[0], tile_size) == 1) & (ctx_rank != anchor_block)
    near_visible = (expand_tiles(tile_mask[0], tile_size) == 1) & (
        row_offsets[None, :] <= row_offsets[:, None]
    )
    visible = jnp.concatenate([far_visible, near_visible], 1)[None]
    scores = jnp.where(visible, scores, jnp.float32(-1e30))
    largest = jnp.max(scores, -1, keepdims=True)
    weights = jnp.where(visible, jnp.exp(scores - largest), jnp.float32(0.0))
    row_total = jnp.sum(weights, -1)
    rounded = weights.astype(jnp.bfloat16)
    attended = (
        jnp.einsum("htk,kd->thd", rounded, all_values, preferred_element_type=jnp.float32)
        / jnp.transpose(row_total)[:, :, None]
    )
    attended = attended.astype(jnp.bfloat16).reshape(block_rows, -1)
    out_rows = lax.all_gather(out_weight, "ctx", axis=1, tiled=True)
    return lax.psum_scatter(
        jnp.dot(attended, out_rows, preferred_element_type=jnp.float32).astype(jnp.bfloat16),
        "zero",
        scatter_dimension=0,
        tiled=True,
    )


def solution(mesh):
    placed = (
        P("ctx", "zero"),
        P(),
        P("ctx", "zero"),
        P("ctx", "zero", None),
        P("zero", "ctx"),
        P("ctx", None, None),
        P("ctx", None, None),
        P(),
    )
    return jax.shard_map(
        local, mesh=mesh, in_specs=placed, out_specs=P(("ctx", "zero"), None), check_vma=False
    )
```

profile of v0, /device:TPU:32, one launch (start us, length us, event | category | flops | bytes accessed | tf_op | source)
XLA Modules:
  0.0 865.7 jit_solution(16125754676907653811)
XLA Ops:
  6.5 0.0 all-gather.6.cloned.1.call-start
  6.5 0.7 all-gather.6.cloned.1.call-update
  7.3 0.0 all-gather.12.cloned.1.call-start
  7.3 0.7 all-gather.12.cloned.1.call-update
  8.0 0.0 all-gather.8.cloned.1.call-start
  8.1 0.7 all-gather.8.cloned.1.call-update
  8.7 0.0 all-reduce.2.cloned.1.call-start
  8.8 0.7 convert_element_type.33
  9.5 76.8 %all-gather.6.cloned.1.call-done = bf16[512,4096]{1,0:T(8,128)(2,1)} async-done(((bf16[512,256]{1,0:T(8,128)(2,1)}), bf16[512,4096]{1,0:T(8,128)(2,1)}) %all-gather.6.cloned.1.call-update) | async-done | bytes 4194320 | tf_op jit(solution)/shard_map/all_gather | solution.py:55
  86.3 3.1 fusion.1
  89.4 0.0 copy-start.1
  89.4 0.0 copy-start
  89.4 127.2 %all-gather.12.cloned.1.call-done = bf16[4096,1,128]{2,0,1:T(8,128)(2,1)} async-done(((bf16[128,1,128]{2,0,1:T(8,128)(2,1)}), bf16[4096,1,128]{2,0,1:T(8,128)(2,1)}) %all-gather.12.cloned.1.call-update) | async-done | bytes 1048592 | tf_op jit(solution)/shard_map/all_gather | solution.py:65
  216.6 4.1 fusion.17
  220.7 0.6 fusion.36
  221.3 1.9 collective-permute-start
  223.9 0.7 collective-permute-done
  224.6 0.7 maximum_select_fusion
  225.3 0.0 all-reduce.2.cloned.1.call-update
  225.3 0.0 all-gather.10.cloned.1.call-start
  225.4 0.5 all-gather.10.cloned.1.call-update
  225.9 0.0 reduce-scatter.2.cloned.1.call-start
  226.0 0.0 copy-done.1
  226.0 0.1 copy.9
  226.1 0.2 broadcast_in_dim.24
  226.3 0.1 copy.24
  226.5 0.0 copy-done
  226.5 0.1 copy.10
  226.6 0.2 broadcast_in_dim.29
  226.8 0.1 fusion.23
  227.0 1.0 multiply_cosine_fusion
  228.0 122.4 %all-gather.8.cloned.1.call-done = bf16[4096,256]{1,0:T(8,128)(2,1)} async-done(((bf16[128,256]{1,0:T(8,128)(2,1)}), bf16[4096,256]{1,0:T(8,128)(2,1)}) %all-gather.8.cloned.1.call-update) | async-done | bytes 2097168 | tf_op jit(solution)/shard_map/all_gather | solution.py:64
  350.4 4.4 fusion.15
  354.9 0.2 copy.18
  355.1 0.2 copy.19
  355.3 0.1 multiply_subtract_fusion
  355.4 260.9 %all-reduce.2.cloned.1.call-done = bf16[2,512,128]{1,2,0:T(8,128)(2,1)} async-done(((bf16[2,512,128]{1,2,0:T(8,128)(2,1)}), bf16[2,512,128]{1,2,0:T(8,128)(2,1)}) %all-reduce.2.cloned.1.call-update) | async-done | bytes 262160 | tf_op jit(solution)/shard_map/psum | solution.py:15
  616.3 1.0 slice_bitcast_fusion.1
  617.2 3.5 fusion.45
  620.7 2.0 fusion.19
  622.8 129.2 %all-gather.10.cloned.1.call-done = bf16[256,4096]{1,0:T(8,128)(2,1)} async-done(((bf16[256,128]{1,0:T(8,128)(2,1)}), bf16[256,4096]{1,0:T(8,128)(2,1)}) %all-gather.10.cloned.1.call-update) | async-done | bytes 2097168 | tf_op jit(solution)/shard_map/all_gather | solution.py:99
  752.0 4.8 convolution_convert_fusion
  756.8 0.0 reduce-scatter.2.cloned.1.call-update
  756.9 102.0 %reduce-scatter.2.cloned.1.call-done = bf16[32,4096]{1,0:T(8,128)(2,1)} async-done(((bf16[512,4096]{1,0:T(8,128)(2,1)}), bf16[32,4096]{1,0:T(8,128)(2,1)}) %reduce-scatter.2.cloned.1.call-update) | async-done | bytes 262160 | tf_op jit(solution)/shard_map/reduce_scatter | solution.py:100
  (9 shorter events, 0.2 us)
Async XLA Ops:
  6.5 79.8 %all-gather.6.cloned.1.call-start = ((), (), s32[]{:S(2)}) async-start(), calls=%async_computation.1 | async-start | bytes 4456448 | tf_op jit(solution)/shard_map/all_gather | solution.py:55
  7.3 209.4 %all-gather.12.cloned.1.call-start = ((), (), s32[]{:S(2)}) async-start(), calls=%async_computation.6 | async-start | bytes 1081344 | tf_op jit(solution)/shard_map/all_gather | solution.py:65
  8.0 342.4 %all-gather.8.cloned.1.call-start = ((), (), s32[]{:S(2)}) async-start(), calls=%async_computation.3 | async-start | bytes 2162688 | tf_op jit(solution)/shard_map/all_gather | solution.py:64
  8.7 607.5 %all-reduce.2.cloned.1.call-start = ((), (), s32[]{:S(2)}) async-start(), calls=%async_computation.2 | async-start | bytes 524288 | tf_op jit(solution)/shard_map/psum | solution.py:15
  89.4 136.6 %copy-start.1 = (s32[1,4,4]{2,1,0:T(4,128)S(1)}, s32[1,4,4]{2,1,0:T(4,128)}, u32[]{:S(2)}) copy-start(s32[1,4,4]{2,1,0:T(4,128)} %param.14) | copy-start | bytes 196
  89.4 137.0 %copy-start = (s32[1,4,4]{2,1,0:T(4,128)S(1)}, s32[1,4,4]{2,1,0:T(4,128)}, u32[]{:S(2)}) copy-start(s32[1,4,4]{2,1,0:T(4,128)} %param.13) | copy-start | bytes 196
  221.3 3.2 collective-permute-start
  225.3 526.7 %all-gather.10.cloned.1.call-start = ((), (), s32[]{:S(2)}) async-start(), calls=%async_computation.4 | async-start | bytes 2162688 | tf_op jit(solution)/shard_map/all_gather | solution.py:99
  225.9 632.9 %reduce-scatter.2.cloned.1.call-start = ((), (), s32[]{:S(2)}) async-start(), calls=%async_computation.5 | async-start | bytes 4456448 | tf_op jit(solution)/shard_map/reduce_scatter | solution.py:100
Sparse Core Ops, SparseCore 0:
  10.5 75.8 all-gather.5
  88.4 128.1 all-gather.11
  218.7 131.6 all-gather.7
  353.1 263.0 all-reduce.1
  618.1 133.8 all-gather.9
  757.0 101.8 reduce-scatter.1
where the time goes:
time: 866 us
  waiting for transfers between devices  822 us (95%)
  matrix products  18.9 us (2%)
  between operations  14.3 us (2%)
    psum x1, waiting for transfers between devices, from_root(): return lax.psum(block, axis)  261 us
    all_gather x1, waiting for transfers between devices, local(): out_rows = lax.all_gather(out_weight, 'ctx', axis=1, tiled=True)  129 us
    all_gather x1, waiting for transfers between devices, local(): lax.all_gather(kv_rows_local, 'ctx', axis=0, tiled=True)  127 us
    all_gather x1, waiting for transfers between devices, local(): lax.all_gather(query_weight, 'ctx', axis=0, tiled=True)  122 us
    reduce_scatter x1, waiting for transfers between devices, local(): lax.psum_scatter(jnp.dot(attended, out_rows, preferred_element_type=jnp.f...  102 us
    all_gather x1, waiting for transfers between devices, local(): gathered = lax.all_gather(activations, 'zero', axis=1, tiled=True)  76.8 us
  transfers between devices with their start and end apart: 7, of which 7 were waited for; matrix products, arithmetic and copies ran while one was open for 3% of the time, Pallas kernels for 0%

commit v1 on v0

--- a/solution.py
+++ b/solution.py
@@ -47,6 +47,15 @@
     anchor_mask,
     anchor_index,
 ):
+
+    def mark_grid(named_axis, packet, pos_dim):
+        return jnp.concatenate(
+            lax.all_to_all(
+                jnp.stack([packet] * lax.axis_size(named_axis), axis=0), named_axis, 0, 0
+            ),
+            pos_dim,
+        )
+
     block_rows = activations.shape[0]
     head_size = kv_weight.shape[2]
     zero_rank = lax.axis_index("zero")
@@ -62,7 +71,7 @@
         return jnp.dot(normed, piece_rows, preferred_element_type=jnp.float32)
 
     query_linear = add_one(lax.all_gather(query_weight, "ctx", axis=0, tiled=True))
-    kv_linear = add_one(lax.all_gather(kv_rows_local, "ctx", axis=0, tiled=True))
+    kv_linear = add_one(mark_grid("ctx", kv_rows_local, 0))
     positions = ctx_rank * block_rows + jnp.arange(block_rows, dtype=jnp.int32)
     queries = (
         rotate(query_linear.reshape(block_rows, -1, head_size), positions) * head_size ** (-0.5)

time: 866 us -> 736 us (0.85)
  waiting for transfers between devices: 822 us -> 674 us
  starting transfers between devices: 2.12 us -> 18.6 us
    all_gather x1 -> x0, waiting for transfers between devices: 127 us -> none  [local(): lax.all_gather(kv_rows_local, 'ctx', axis=0, tiled=True)]
    all_to_all x0 -> x1, starting transfers between devices: none -> 16.3 us  [mark_grid(): lax.all_to_all(jnp.stack([packet] * lax.axis_size(named_axis), axis=0), n...]
    all_gather x1, waiting for transfers between devices: 76.8 us -> 61.6 us  [local(): gathered = lax.all_gather(activations, 'zero', axis=1, tiled=True)]
  transfers between devices with their start and end apart: 7 -> 7, of which waited for: 7 -> 6; matrix products, arithmetic and copies ran while one was open for 3% -> 3% of each run, Pallas kernels for 0% -> 0%
where the time goes in v1:
time: 736 us
  waiting for transfers between devices  674 us (92%)
  starting transfers between devices  18.6 us (3%)
  matrix products  18.6 us (3%)
  between operations  14 us (2%)
    psum x1, waiting for transfers between devices, from_root(): return lax.psum(block, axis)  261 us
    all_gather x1, waiting for transfers between devices, local(): out_rows = lax.all_gather(out_weight, 'ctx', axis=1, tiled=True)  129 us
    all_gather x1, waiting for transfers between devices, local(): lax.all_gather(query_weight, 'ctx', axis=0, tiled=True)  118 us
    reduce_scatter x1, waiting for transfers between devices, local(): lax.psum_scatter(jnp.dot(attended, out_rows, preferred_element_type=jnp.f...  102 us
    all_gather x1, waiting for transfers between devices, local(): gathered = lax.all_gather(activations, 'zero', axis=1, tiled=True)  61.6 us
    all_to_all x1, starting transfers between devices, mark_grid(): lax.all_to_all(jnp.stack([packet] * lax.axis_size(named_axis), axis=0), n...  16.3 us
  transfers between devices with their start and end apart: 7, of which 6 were waited for; matrix products, arithmetic and copies ran while one was open for 3% of the time, Pallas kernels for 0%

profile of v1, /device:TPU:32, one launch (start us, length us, event | category | flops | bytes accessed | tf_op | source)
XLA Modules:
  0.0 735.9 jit_solution(4992441169461607743)
XLA Ops:
  6.5 0.0 all-gather.4.cloned.1.call-start
  6.5 0.7 all-gather.4.cloned.1.call-update
  7.3 2.0 stack.12
  9.2 16.3 %all-to-all-start = ((bf16[32,128,128]{2,1,0:T(8,128)(2,1)}), bf16[32,128,128]{2,1,0:T(8,128)(2,1)S(1)}, u32[]{:S(2)}, u32[]{:S(2)}) async-start(bf16[32,128,128]{2,1,0:T(8,128)(2,1)} %stack.12), calls=%async_computation | async-start | bytes 2097152 | tf_op jit(solution)/shard_map/all_to_all | solution.py:53
  25.5 0.0 all-gather.6.cloned.1.call-start
  25.6 0.7 all-gather.6.cloned.1.call-update
  26.3 0.0 all-reduce.2.cloned.1.call-start
  26.3 0.7 convert_element_type.33
  27.0 61.6 %all-gather.4.cloned.1.call-done = bf16[512,4096]{1,0:T(8,128)(2,1)} async-done(((bf16[512,256]{1,0:T(8,128)(2,1)}), bf16[512,4096]{1,0:T(8,128)(2,1)}) %all-gather.4.cloned.1.call-update) | async-done | bytes 4194320 | tf_op jit(solution)/shard_map/all_gather | solution.py:64
  88.6 3.1 fusion.1
  91.7 0.0 all-to-all-done
  91.7 0.0 copy-start.1
  91.7 0.0 copy-start
  91.8 3.8 fusion.17
  95.6 0.6 fusion.35
  96.2 2.2 collective-permute-start
  99.0 0.4 collective-permute-done
  99.4 0.7 maximum_select_fusion
  100.2 0.0 all-reduce.2.cloned.1.call-update
  100.2 0.0 all-gather.8.cloned.1.call-start
  100.2 0.5 all-gather.8.cloned.1.call-update
  100.8 0.0 reduce-scatter.2.cloned.1.call-start
  100.8 0.0 copy-done.1
  100.8 0.1 copy.9
  101.0 0.2 broadcast_in_dim.24
  101.2 0.1 copy.24
  101.3 0.0 copy-done
  101.3 0.1 copy.10
  101.4 0.2 broadcast_in_dim.29
  101.7 0.1 fusion.22
  101.8 1.0 multiply_cosine_fusion
  102.8 117.8 %all-gather.6.cloned.1.call-done = bf16[4096,256]{1,0:T(8,128)(2,1)} async-done(((bf16[128,256]{1,0:T(8,128)(2,1)}), bf16[4096,256]{1,0:T(8,128)(2,1)}) %all-gather.6.cloned.1.call-update) | async-done | bytes 2097168 | tf_op jit(solution)/shard_map/all_gather | solution.py:73
  220.7 4.4 fusion.15
  225.1 0.2 copy.18
  225.3 0.2 copy.19
  225.5 0.1 multiply_subtract_fusion
  225.7 261.0 %all-reduce.2.cloned.1.call-done = bf16[2,512,128]{1,2,0:T(8,128)(2,1)} async-done(((bf16[2,512,128]{1,2,0:T(8,128)(2,1)}), bf16[2,512,128]{1,2,0:T(8,128)(2,1)}) %all-reduce.2.cloned.1.call-update) | async-done | bytes 262160 | tf_op jit(solution)/shard_map/psum | solution.py:15
  486.7 1.0 slice_bitcast_fusion.1
  487.7 3.5 fusion.44
  491.2 2.0 fusion.19
  493.2 129.2 %all-gather.8.cloned.1.call-done = bf16[256,4096]{1,0:T(8,128)(2,1)} async-done(((bf16[256,128]{1,0:T(8,128)(2,1)}), bf16[256,4096]{1,0:T(8,128)(2,1)}) %all-gather.8.cloned.1.call-update) | async-done | bytes 2097168 | tf_op jit(solution)/shard_map/all_gather | solution.py:108
  622.5 4.8 convolution_convert_fusion
  627.3 0.0 reduce-scatter.2.cloned.1.call-update
  627.3 102.0 %reduce-scatter.2.cloned.1.call-done = bf16[32,4096]{1,0:T(8,128)(2,1)} async-done(((bf16[512,4096]{1,0:T(8,128)(2,1)}), bf16[32,4096]{1,0:T(8,128)(2,1)}) %reduce-scatter.2.cloned.1.call-update) | async-done | bytes 262160 | tf_op jit(solution)/shard_map/reduce_scatter | solution.py:109
  (9 shorter events, 0.2 us)
Async XLA Ops:
  6.5 82.1 %all-gather.4.cloned.1.call-start = ((), (), s32[]{:S(2)}) async-start(), calls=%async_computation.2 | async-start | bytes 4456448 | tf_op jit(solution)/shard_map/all_gather | solution.py:64
  9.2 82.5 %all-to-all-start = ((bf16[32,128,128]{2,1,0:T(8,128)(2,1)}), bf16[32,128,128]{2,1,0:T(8,128)(2,1)S(1)}, u32[]{:S(2)}, u32[]{:S(2)}) async-start(bf16[32,128,128]{2,1,0:T(8,128)(2,1)} %stack.12), calls=%async_computation | async-start | bytes 2097152 | tf_op jit(solution)/shard_map/all_to_all | solution.py:53
  25.5 195.1 %all-gather.6.cloned.1.call-start = ((), (), s32[]{:S(2)}) async-start(), calls=%async_computation.4 | async-start | bytes 2162688 | tf_op jit(solution)/shard_map/all_gather | solution.py:73
  26.3 460.4 %all-reduce.2.cloned.1.call-start = ((), (), s32[]{:S(2)}) async-start(), calls=%async_computation.3 | async-start | bytes 524288 | tf_op jit(solution)/shard_map/psum | solution.py:15
  91.7 9.1 %copy-start.1 = (s32[1,4,4]{2,1,0:T(4,128)S(1)}, s32[1,4,4]{2,1,0:T(4,128)}, u32[]{:S(2)}) copy-start(s32[1,4,4]{2,1,0:T(4,128)} %param.14) | copy-start | bytes 196
  91.7 9.6 %copy-start = (s32[1,4,4]{2,1,0:T(4,128)S(1)}, s32[1,4,4]{2,1,0:T(4,128)}, u32[]{:S(2)}) copy-start(s32[1,4,4]{2,1,0:T(4,128)} %param.13) | copy-start | bytes 196
  96.2 3.2 collective-permute-start
  100.2 522.3 %all-gather.8.cloned.1.call-start = ((), (), s32[]{:S(2)}) async-start(), calls=%async_computation.5 | async-start | bytes 2162688 | tf_op jit(solution)/shard_map/all_gather | solution.py:108
  100.8 628.6 %reduce-scatter.2.cloned.1.call-start = ((), (), s32[]{:S(2)}) async-start(), calls=%async_computation.6 | async-start | bytes 4456448 | tf_op jit(solution)/shard_map/reduce_scatter | solution.py:109
Sparse Core Ops, SparseCore 0:
  10.5 78.1 all-gather.3
  90.7 129.8 all-gather.5
  223.6 263.0 all-reduce.1
  488.6 133.8 all-gather.7
  627.5 101.8 reduce-scatter.1
